TPU v7x, 32 devices: a whole 2x2x4 slice. The times are simulated.
32 devices in a mesh: frow: 16 (over z, y, core), fcol: 2 (over x).
Axes of the slice: x: 2, y: 2, z: 4, core: 2. Of those that a mesh axis runs over, the one named last changes fastest.
Arguments:
- face_input: bfloat16 [12, 64, 64, 256], P(None, 'frow', 'fcol'), may hold values from -6 to 6
- kernel: bfloat16 [3, 3, 256, 256], replicated, may hold values from -0.125 to 0.125
- convolution_bias: float32 [256], replicated, may hold values from -3 to 3
- upstream: bfloat16 [12, 64, 64, 256], P(None, 'frow', 'fcol'), may hold values from -6 to 6
- adjacency: int32 [12, 4, 3], replicated, may hold values from 0 to 11, as said below
Outputs:
- activation: bfloat16 [12, 64, 64, 256], P(None, 'frow', 'fcol')
- input_gradient: bfloat16 [12, 64, 64, 256], P(None, 'frow', 'fcol')
- kernel_grad: float32 [3, 3, 256, 256], replicated
- bias_grad: float32 [256], replicated
Inputs may be any that keep to these rules, and one draw needn't show every extreme that they name: adjacency[f, s] = (g, t, r): side s of face f (0 top, 1 bottom, 2 left, 3 right) borders side t of face g; t is 0 or 1 exactly when s is; r = 1 when positions along the seam run in opposite directions, else 0; the relation is symmetric, adjacency[g, t] = (f, s, r), and no side borders itself.
All inputs are finite; a program needn't handle non-finite values.
Results may differ from a plain program's by a relative error of at most 0.018.
Values may be sent and summed in bfloat16 or wider, within the bound.
No kernel may reach another device: no remote copies, remote signals or barrier semaphores. Data moves between devices by JAX's collectives and lax.ppermute only.
A program may use at most 128 MiB of HBM per device.

v0:
```python
import math
import jax
import jax.numpy as jnp
from jax import lax
from jax.sharding import PartitionSpec as P

DILATION_STEP = 2
half_root = 0.7071067811865476
density_scale = 0.3989422804014327


def from_partner(value, axis, distance):
    return lax.ppermute(value, axis, [(i, i ^ 1 << distance) for i in range(lax.axis_size(axis))])


def with_halo(block, sides, width):
    for axis, dim in sides:
        count = lax.axis_size(axis)
        forward = [(i, i + 1) for i in range(count - 1)]
        forward.append((count - 1, 0))
        backward = [(target, source) for source, target in forward]
        low = lax.ppermute(
            lax.slice_in_dim(block, block.shape[dim] - width, None, axis=dim), axis, forward
        )
        high = lax.ppermute(lax.slice_in_dim(block, 0, width, axis=dim), axis, backward)
        block = jnp.concatenate([low, block, high], axis=dim)
    return block


def gelu_value(value):
    return 0.5 * value * (1.0 + jax.scipy.special.erf(value * half_root))


def gelu_slope(value):
    return (
        0.5 * (1.0 + jax.scipy.special.erf(value * half_root))
        + value * jnp.exp(-0.5 * value * value) * density_scale
    )


def pick_table(entries, side_near, face_count):
    same_side = (entries[:, 1] == side_near).astype(jnp.int32)
    slot_index = (2 * entries[:, 2] + same_side) * face_count + entries[:, 0]
    return (slot_index[:, None] == jnp.arange(4 * face_count, dtype=jnp.int32)[None, :]).astype(
        jnp.bfloat16
    )


def reflect(row_band, col_band, returning):
    col_bits = lax.axis_size("fcol").bit_length() - 1
    all_bits = (lax.axis_size("frow") * lax.axis_size("fcol")).bit_length() - 1
    for bit_index in range(all_bits):
        moving = row_band if bit_index < col_bits else col_band
        if returning:
            moved = from_partner(moving, ("frow", "fcol"), bit_index)
        else:
            moved = from_partner(moving, ("frow", "fcol"), bit_index)
        if bit_index < col_bits:
            row_band = moved
        else:
            col_band = moved
    return (row_band, col_band)


def fold_border(extended, along, cells, inner_size):
    middle = lax.slice_in_dim(extended, 2 * cells, 2 * cells + inner_size, axis=along)
    before = lax.slice_in_dim(extended, 0, cells, axis=along)
    after_rim = lax.slice_in_dim(
        extended, inner_size + 3 * cells, inner_size + 4 * cells, axis=along
    )
    lead_pads = [(0, 0)] * extended.ndim
    tail_pads = [(0, 0)] * extended.ndim
    lead_pads[along] = (0, inner_size - cells)
    tail_pads[along] = (inner_size - cells, 0)
    return middle + jnp.pad(before, lead_pads) + jnp.pad(after_rim, tail_pads)


def local(face_input, kernel, convolution_bias, upstream, adjacency):
    face_count = face_input.shape[0]
    tile_rows = face_input.shape[1]
    tile_cols = face_input.shape[2]
    dilation_step = DILATION_STEP
    height = tile_rows + 2 * dilation_step
    breadth = tile_cols + 2 * dilation_step
    at_top = lax.axis_index("frow") == 0
    at_bottom = lax.axis_index("frow") == lax.axis_size("frow") - 1
    at_left = lax.axis_index("fcol") == 0
    at_right = lax.axis_index("fcol") == lax.axis_size("fcol") - 1
    column_index = jnp.arange(breadth)
    keep_cols = jnp.logical_not(
        at_left & (column_index < dilation_step)
        | at_right & (column_index >= tile_cols + dilation_step)
    )
    row_index = jnp.arange(height)
    keep_rows = jnp.logical_not(
        at_top & (row_index < dilation_step) | at_bottom & (row_index >= tile_rows + dilation_step)
    )
    padded_input = with_halo(face_input, (("frow", 1), ("fcol", 2)), dilation_step)
    row_wrap = jnp.where(
        at_top, padded_input[:, :dilation_step], padded_input[:, tile_rows + dilation_step :]
    )
    row_own = jnp.where(
        at_top,
        padded_input[:, dilation_step : 2 * dilation_step],
        padded_input[:, tile_rows : tile_rows + dilation_step],
    )
    col_wrap = jnp.where(
        at_left, padded_input[:, :, :dilation_step], padded_input[:, :, tile_cols + dilation_step :]
    )
    col_own = jnp.where(
        at_left,
        padded_input[:, :, dilation_step : 2 * dilation_step],
        padded_input[:, :, tile_cols : tile_cols + dilation_step],
    )
    row_send = jnp.concatenate([row_wrap, row_own], 1)
    col_send = jnp.concatenate([col_wrap, col_own], 2)
    far_rows, far_cols = reflect(row_send, col_send, False)
    row_pick = pick_table(
        jnp.where(at_top, adjacency[:, 0], adjacency[:, 1]), jnp.where(at_top, 0, 1), face_count
    )
    col_pick = pick_table(
        jnp.where(at_left, adjacency[:, 2], adjacency[:, 3]), jnp.where(at_left, 2, 3), face_count
    )
    row_cands = jnp.concatenate(
        [
            row_wrap,
            jnp.flip(row_own, 1),
            jnp.flip(far_rows[:, :dilation_step], 2),
            jnp.flip(far_rows[:, dilation_step:], (1, 2)),
        ],
        0,
    )
    row_halo = jnp.einsum("fk,kdwc->fdwc", row_pick, row_cands, preferred_element_type=jnp.float32)
    row_halo = jnp.where(keep_cols[None, None, :, None], row_halo, 0.0).astype(jnp.bfloat16)
    top_rim = jnp.where(at_top, row_halo, padded_input[:, :dilation_step])
    bottom_rim = jnp.where(at_bottom, row_halo, padded_input[:, tile_rows + dilation_step :])
    padded_input = jnp.concatenate(
        [top_rim, padded_input[:, dilation_step : tile_rows + dilation_step], bottom_rim], 1
    )
    col_cands = jnp.concatenate(
        [
            col_wrap,
            jnp.flip(col_own, 2),
            jnp.flip(far_cols[:, :, :dilation_step], 1),
            jnp.flip(far_cols[:, :, dilation_step:], (1, 2)),
        ],
        0,
    )
    col_halo = jnp.einsum("fk,kadc->fadc", col_pick, col_cands, preferred_element_type=jnp.float32)
    col_halo = jnp.where(keep_rows[None, :, None, None], col_halo, 0.0).astype(jnp.bfloat16)
    left_rim = jnp.where(at_left, col_halo, padded_input[:, :, :dilation_step])
    right_rim = jnp.where(at_right, col_halo, padded_input[:, :, tile_cols + dilation_step :])
    padded_input = jnp.concatenate(
        [left_rim, padded_input[:, :, dilation_step : tile_cols + dilation_step], right_rim], 2
    )
    random_values = ("NHWC", "HWIO", "NHWC")
    preactivation = (
        lax.conv_general_dilated(
            padded_input,
            kernel,
            (1, 1),
            "VALID",
            rhs_dilation=(dilation_step, dilation_step),
            dimension_numbers=random_values,
            preferred_element_type=jnp.float32,
        )
        + convolution_bias
    )
    activation = gelu_value(preactivation).astype(jnp.bfloat16)
    preactivation_gradient = (upstream.astype(jnp.float32) * gelu_slope(preactivation)).astype(
        jnp.bfloat16
    )
    tap_list = []
    for kernel_row_offset in range(3):
        for kernel_column_offset in range(3):
            input_window = padded_input[
                :,
                kernel_row_offset * dilation_step : kernel_row_offset * dilation_step + tile_rows,
                kernel_column_offset * dilation_step : kernel_column_offset * dilation_step
                + tile_cols,
            ]
            tap_list.append(
                lax.dot_general(
                    input_window,
                    preactivation_gradient,
                    (((0, 1, 2), (0, 1, 2)), ((), ())),
                    preferred_element_type=jnp.float32,
                )
            )
    kernel_local = jnp.stack(tap_list, 0).reshape(kernel.shape)
    bias_local = jnp.sum(preactivation_gradient.astype(jnp.float32), axis=(0, 1, 2))
    kernel_total, bias_total = lax.psum((kernel_local, bias_local), ("frow", "fcol"))
    scale = 1.0 / math.sqrt(
        face_count * tile_rows * lax.axis_size("frow") * tile_cols * lax.axis_size("fcol")
    )
    kernel_grad = kernel_total * scale
    bias_grad = bias_total * scale
    rotated_strip = jnp.transpose(jnp.flip(kernel, (0, 1)), (0, 1, 3, 2))
    twice = 2 * dilation_step
    padded_gradient = lax.conv_general_dilated(
        preactivation_gradient,
        rotated_strip,
        (1, 1),
        ((twice, twice), (twice, twice)),
        rhs_dilation=(dilation_step, dilation_step),
        dimension_numbers=random_values,
        preferred_element_type=jnp.float32,
    ).astype(jnp.bfloat16)
    row_seam = jnp.where(
        at_top, padded_gradient[:, :dilation_step], padded_gradient[:, tile_rows + dilation_step :]
    )
    row_seam = jnp.where(keep_cols[None, None, :, None], row_seam, jnp.zeros_like(row_seam))
    row_split = jnp.einsum("fk,fdwc->kdwc", row_pick, row_seam, preferred_element_type=jnp.float32)
    row_split = row_split.reshape((4, face_count) + row_split.shape[1:])
    col_seam = jnp.where(
        at_left,
        padded_gradient[:, :, :dilation_step],
        padded_gradient[:, :, tile_cols + dilation_step :],
    )
    col_seam = jnp.where(keep_rows[None, :, None, None], col_seam, jnp.zeros_like(col_seam))
    col_split = jnp.einsum("fk,fadc->kadc", col_pick, col_seam, preferred_element_type=jnp.float32)
    col_split = col_split.reshape((4, face_count) + col_split.shape[1:])
    row_far_grad = jnp.concatenate(
        [jnp.flip(row_split[2], 2), jnp.flip(row_split[3], (1, 2))], 1
    ).astype(jnp.bfloat16)
    col_far_grad = jnp.concatenate(
        [jnp.flip(col_split[2], 1), jnp.flip(col_split[3], (1, 2))], 2
    ).astype(jnp.bfloat16)
    row_back, col_back = reflect(row_far_grad, col_far_grad, True)
    wrap_rows = row_split[0] + row_back[:, :dilation_step].astype(jnp.float32)
    own_rows = jnp.flip(row_split[1], 1) + row_back[:, dilation_step:].astype(jnp.float32)
    wrap_cols = col_split[0] + col_back[:, :, :dilation_step].astype(jnp.float32)
    own_cols = jnp.flip(col_split[1], 2) + col_back[:, :, dilation_step:].astype(jnp.float32)
    gathered = padded_gradient.astype(jnp.float32)
    middle_rows = gathered[:, dilation_step : tile_rows + dilation_step]
    middle_rows = middle_rows + jnp.pad(
        jnp.where(at_top, own_rows, 0.0), ((0, 0), (0, tile_rows - dilation_step), (0, 0), (0, 0))
    )
    middle_rows = middle_rows + jnp.pad(
        jnp.where(at_bottom, own_rows, 0.0),
        ((0, 0), (tile_rows - dilation_step, 0), (0, 0), (0, 0)),
    )
    top_grad = jnp.where(at_top, wrap_rows, gathered[:, :dilation_step])
    bottom_grad = jnp.where(at_bottom, wrap_rows, gathered[:, tile_rows + dilation_step :])
    gathered = jnp.concatenate([top_grad, middle_rows, bottom_grad], 1)
    middle_cols = gathered[:, :, dilation_step : tile_cols + dilation_step]
    middle_cols = middle_cols + jnp.pad(
        jnp.where(at_left, own_cols, 0.0), ((0, 0), (0, 0), (0, tile_cols - dilation_step), (0, 0))
    )
    middle_cols = middle_cols + jnp.pad(
        jnp.where(at_right, own_cols, 0.0), ((0, 0), (0, 0), (tile_cols - dilation_step, 0), (0, 0))
    )
    left_grad = jnp.where(at_left, wrap_cols, gathered[:, :, :dilation_step])
    right_grad = jnp.where(at_right, wrap_cols, gathered[:, :, tile_cols + dilation_step :])
    gathered = jnp.concatenate([left_grad, middle_cols, right_grad], 2)
    returned = with_halo(
        gathered.astype(jnp.bfloat16), (("frow", 1), ("fcol", 2)), dilation_step
    ).astype(gathered.dtype)
    folded = fold_border(returned, 1, dilation_step, tile_rows)
    folded = fold_border(folded, 2, dilation_step, tile_cols)
    input_gradient = folded.astype(jnp.bfloat16)
    return (activation, input_gradient, kernel_grad, bias_grad)


def solution(mesh):
    return jax.shard_map(
        local,
        mesh=mesh,
        in_specs=(P(None, "frow", "fcol", None), P(), P(), P(None, "frow", "fcol", None), P()),
        out_specs=(P(None, "frow", "fcol", None), P(None, "frow", "fcol", None), P(), P()),
        check_vma=False,
    )
```

profile of v0, /device:TPU:0, one launch (start us, length us, event | category | flops | bytes accessed | tf_op | source)
XLA Modules:
  0.0 288.5 jit_solution(14397074329144345583)
XLA Ops:
  7.2 1.3 fusion.113
  9.5 5.1 %collective-permute-start.1 = (bf16[12,2,32,256]{3,0,2,1:T(8,128)(2,1)S(1)}, bf16[12,2,32,256]{3,0,2,1:T(8,128)(2,1)}, u32[]{:S(2)}, u32[]{:S(2)}) collective-permute-start(bf16[12,2,32,256]{3,0,2,1:T(8,128)(2,1)S(1)} %copy.171), channel_id=1, source_target_pairs={{2,0},{4,2},{6,4},{8,6},{10,8},{12,10},{14,12},{16,14},{18,16},{20... | collective-permute-start | bytes 1179656 | tf_op jit(solution)/shard_map/ppermute | solution.py:25
  14.6 6.8 %collective-permute-done = bf16[12,2,32,256]{3,0,2,1:T(8,128)(2,1)} collective-permute-done((bf16[12,2,32,256]{3,0,2,1:T(8,128)(2,1)S(1)}, bf16[12,2,32,256]{3,0,2,1:T(8,128)(2,1)}, u32[]{:S(2)}, u32[]{:S(2)}) %collective-permute-start) | collective-permute-done | bytes 393248 | tf_op jit(solution)/shard_map/ppermute | solution.py:22
  21.4 1.1 constant_dynamic-update-slice_fusion.2
  22.9 1.1 constant_dynamic-update-slice_fusion
  24.0 1.3 copy-done.5
  25.4 2.0 collective-permute-start.3
  27.5 2.9 %collective-permute-done.3 = bf16[12,8,2,256]{3,0,2,1:T(8,128)(2,1)S(1)} collective-permute-done((bf16[12,8,2,256]{3,0,2,1:T(8,128)(2,1)S(1)}, bf16[12,8,2,256]{3,0,2,1:T(8,128)(2,1)S(1)}, u32[]{:S(2)}, u32[]{:S(2)}) %collective-permute-start.3) | collective-permute-done | bytes 98336 | tf_op jit(solution)/shard_map/ppermute | solution.py:25
  30.4 2.7 collective-permute-done.2
  33.1 2.0 collective-permute-start.4
  35.1 1.9 pad_maximum_fusion.1
  37.3 1.1 copy-done.2
  38.4 1.6 copy.94
  40.1 1.4 collective-permute-start.8
  41.5 1.7 collective-permute-start.5
  43.2 6.7 %collective-permute-done.5 = bf16[12,8,4,256]{3,0,2,1:T(8,128)(2,1)S(1)} collective-permute-done((bf16[12,8,4,256]{3,0,2,1:T(8,128)(2,1)S(1)}, bf16[12,8,4,256]{3,0,2,1:T(8,128)(2,1)S(1)}, u32[]{:S(2)}, u32[]{:S(2)}) %collective-permute-start.5) | collective-permute-done | bytes 196640 | tf_op jit(solution)/shard_map/ppermute | solution.py:13
  49.9 1.6 collective-permute-start.6
  51.5 6.3 %collective-permute-done.6 = bf16[12,8,4,256]{3,0,2,1:T(8,128)(2,1)S(1)} collective-permute-done((bf16[12,8,4,256]{3,0,2,1:T(8,128)(2,1)S(1)}, bf16[12,8,4,256]{3,0,2,1:T(8,128)(2,1)S(1)}, u32[]{:S(2)}, u32[]{:S(2)}) %collective-permute-start.6) | collective-permute-done | bytes 196640 | tf_op jit(solution)/shard_map/ppermute | solution.py:13
  57.7 2.8 collective-permute-start.7
  60.5 0.7 rev.50
  61.2 1.3 slice.305
  62.5 1.9 rev.53
  64.4 7.3 %collective-permute-done.7 = bf16[12,8,4,256]{3,0,2,1:T(8,128)(2,1)} collective-permute-done((bf16[12,8,4,256]{3,0,2,1:T(8,128)(2,1)S(1)}, bf16[12,8,4,256]{3,0,2,1:T(8,128)(2,1)}, u32[]{:S(2)}, u32[]{:S(2)}) %collective-permute-start.7) | collective-permute-done | bytes 196640 | tf_op jit(solution)/shard_map/ppermute | solution.py:13
  71.7 1.0 fusion.114
  72.7 0.7 rev.51
  73.4 3.0 %fusion.111 = (bf16[12,2,36,256]{3,1,2,0:T(2,128)(2,1)S(1)}, bf16[12,2,36,256]{3,1,2,0:T(2,128)(2,1)}) fusion(bf16[12,4,36,256]{3,1,2,0:T(4,128)(2,1)} %collective-permute-done.8), kind=kLoop, calls=%fused_computation.185 | loop fusion | bytes 1769472 | tf_op jit(solution)/shard_map/slice | solution.py:128
  76.4 0.9 copy.130
  77.3 1.9 rev.54
  79.2 1.9 copy.131
  81.2 1.9 rev.55
  83.1 2.7 broadcast_select_fusion.1
  85.8 1.2 pad_maximum_fusion.6
  87.5 0.7 copy-done.15
  88.5 2.1 pad_maximum_fusion.5
  90.7 2.8 fusion.5
  93.5 2.6 convert_reduce_fusion
  96.1 8.3 %fusion.115 = (f32[12,8,36,256]{3,0,2,1:T(8,128)}, bf16[12,8,36,256]{3,0,2,1:T(8,128)(2,1)S(1)}) fusion(bf16[3,3,256,256]{3,2,1,0:T(8,128)(2,1)S(1)} %copy-done, bf16[12,4,32,256]{3,2,1,0:T(8,128)(2,1)S(1)} %get-tuple-element.21), kind=kOutput, calls=%fused_computation.189 | convolution fusion | flops 1813708800 | bytes 7274496 | tf_op jit(solution)/shard_map/conv_general_dilated | solution.py:200
  104.8 2.6 fusion.60
  110.0 1.4 copy-done.8
  111.6 2.0 fusion.108
  113.8 1.6 copy.99
  116.0 1.2 fusion.37
  117.3 1.1 collective-permute-start.10
  118.4 1.2 fusion.36
  119.7 6.2 %collective-permute-done.10 = bf16[12,8,4,256]{3,0,2,1:T(8,128)(2,1)S(1)} collective-permute-done((bf16[12,8,4,256]{3,0,2,1:T(8,128)(2,1)}, bf16[12,8,4,256]{3,0,2,1:T(8,128)(2,1)S(1)}, u32[]{:S(2)}, u32[]{:S(2)}) %collective-permute-start.10) | collective-permute-done | bytes 196640 | tf_op jit(solution)/shard_map/ppermute | solution.py:13
  126.5 1.2 fusion.35
  127.7 5.8 %collective-permute-done.11 = bf16[12,8,4,256]{3,0,2,1:T(8,128)(2,1)S(1)} collective-permute-done((bf16[12,8,4,256]{3,0,2,1:T(8,128)(2,1)S(1)}, bf16[12,8,4,256]{3,0,2,1:T(8,128)(2,1)S(1)}, u32[]{:S(2)}, u32[]{:S(2)}) %collective-permute-start.11) | collective-permute-done | bytes 196640 | tf_op jit(solution)/shard_map/ppermute | solution.py:13
  133.6 2.4 collective-permute-start.12
  136.0 1.2 fusion.34
  137.2 12.1 %collective-permute-done.12 = bf16[12,8,4,256]{3,0,2,1:T(8,128)(2,1)S(1)} collective-permute-done((bf16[12,8,4,256]{3,0,2,1:T(8,128)(2,1)S(1)}, bf16[12,8,4,256]{3,0,2,1:T(8,128)(2,1)S(1)}, u32[]{:S(2)}, u32[]{:S(2)}) %collective-permute-start.12) | collective-permute-done | bytes 196640 | tf_op jit(solution)/shard_map/ppermute | solution.py:13
  149.4 2.2 fusion.110
  151.7 3.5 %slice_select_fusion.3 = (f32[12,2,36,256]{3,0,2,1:T(8,128)S(1)}, f32[12,2,36,256]{3,0,2,1:T(8,128)S(1)}, f32[12,2,36,256]{3,0,2,1:T(8,128)S(1)}) fusion(f32[12,8,36,256]{3,0,2,1:T(8,128)} %get-tuple-element.70, f32[48,2,36,256]{3,0,2,1:T(8,128)} %fusion.60, bf16[12,2,36,256]{3,1,2,0:T(2,128)(2,1)S(1)} %get-tuple-element.57, pred[]{:T(512)S(6)} %eq.57, ...), kind=kLoop, calls=%fused_computation.53 | loop fusion | flops 884736 | bytes 6635522 | tf_op jit(solution)/shard_map/jit(_where)/select_n | solution.py:243
  157.5 1.2 copy.103
  158.7 4.1 %collective-permute-start.15 = (bf16[12,2,36,256]{3,1,2,0:T(2,128)(2,1)}, bf16[12,2,36,256]{3,1,2,0:T(2,128)(2,1)S(1)}, u32[]{:S(2)}, u32[]{:S(2)}) collective-permute-start(bf16[12,2,36,256]{3,1,2,0:T(2,128)(2,1)} %copy.103), channel_id=1, source_target_pairs={{2,0},{4,2},{6,4},{8,6},{10,8},{12,10},{14,12},{16,14},{18,16},{20... | collective-permute-start | bytes 1327112 | tf_op jit(solution)/shard_map/ppermute | solution.py:25
  162.9 1.2 copy.102
  164.1 42.6 %psum.15 = f32[256]{0:T(256)S(1)} all-reduce(f32[256]{0:T(256)S(1)} %get-tuple-element.20), channel_id=1, replica_groups=mesh['frow'=16,'fcol'=2] {'frow','fcol'}, use_global_device_ids=true, to_apply=%region_2.3 | all-reduce | flops 256 | bytes 2048 | tf_op jit(solution)/shard_map/psum | solution.py:192
  207.4 1.1 copy.104
  208.5 0.8 pad_maximum_fusion.18
  209.4 2.3 collective-permute-start.16
  211.7 60.8 %all-reduce.8.cloned.1.call-done = f32[3,3,256,256]{3,2,1,0:T(8,128)} async-done(((f32[3,3,256,256]{3,2,1,0:T(8,128)}), f32[3,3,256,256]{3,2,1,0:T(8,128)}) %all-reduce.8.cloned.1.call-update) | async-done | bytes 2359312 | tf_op jit(solution)/shard_map/psum | solution.py:192
  272.5 3.3 %broadcast_multiply_fusion = f32[3,3,256,256]{3,2,1,0:T(8,128)} fusion(f32[3,3,256,256]{3,2,1,0:T(8,128)} %all-reduce.8.cloned.1.call-done), kind=kLoop, calls=%fused_computation.57 | loop fusion | flops 589824 | bytes 4718592 | tf_op jit(solution)/shard_map/mul | solution.py:196
  275.7 2.9 %maximum_convert_fusion = f32[12,12,40,256]{3,0,2,1:T(8,128)S(1)} fusion(bf16[12,12,2,256]{3,0,2,1:T(8,128)(2,1)} %collective-permute-done.17, bf16[12,2,36,256]{3,0,2,1:T(8,128)(2,1)S(1)} %copy.105, bf16[12,8,2,256]{3,0,2,1:T(8,128)(2,1)S(1)} %get-tuple-element.25, bf16[12,8,32,256]{3,0,2,1:T(8,128)(2,1)S(1)} %fusion.1, ...), kind=kLoop, calls=%fused_computation.4 | loop fusion | flops 10321920 | bytes 8847360 | tf_op jit(solution)/shard_map/convert_element_type | solution.py:258
  279.3 0.8 fusion.3
  280.5 1.1 copy.115
  (110 shorter events, 11.6 us)
Async XLA Ops:
  7.2 83.5 %copy-start = (bf16[3,3,256,256]{3,2,1,0:T(8,128)(2,1)S(1)}, bf16[3,3,256,256]{3,2,1,0:T(8,128)(2,1)}, u32[]{:S(2)}) copy-start(bf16[3,3,256,256]{3,2,1,0:T(8,128)(2,1)} %param.6) | copy-start | bytes 3538948
  7.2 15.3 %copy-start.3 = (bf16[12,4,32,256]{3,2,1,0:T(8,128)(2,1)S(1)}, bf16[12,4,32,256]{3,2,1,0:T(8,128)(2,1)}, u32[]{:S(2)}) copy-start(bf16[12,4,32,256]{3,2,1,0:T(8,128)(2,1)} %param.5) | copy-start | bytes 2359300
  7.2 265.3 %all-reduce.8.cloned.1.call-start = ((), (), s32[]{:S(2)}) async-start(), calls=%async_computation | async-start | bytes 4718592 | tf_op jit(solution)/shard_map/psum | solution.py:192
  8.8 12.6 %collective-permute-start = (bf16[12,2,32,256]{3,0,2,1:T(8,128)(2,1)S(1)}, bf16[12,2,32,256]{3,0,2,1:T(8,128)(2,1)}, u32[]{:S(2)}, u32[]{:S(2)}) collective-permute-start(bf16[12,2,32,256]{3,0,2,1:T(8,128)(2,1)S(1)} %copy.170), channel_id=1, source_target_pairs={{0,2},{2,4},{4,6},{6,8},{8,10},{10,12},{12,14},{14,16},{16,18},{18... | collective-permute-start | bytes 1179656 | tf_op jit(solution)/shard_map/ppermute | solution.py:22
  9.5 17.9 %copy-start.17 = (s32[12,4,3]{0,1,2:T(4,128)S(1)}, s32[12,4,3]{0,1,2:T(4,128)}, u32[]{:S(2)}) copy-start(s32[12,4,3]{0,1,2:T(4,128)} %param.9) | copy-start | bytes 1732
  9.5 13.4 %collective-permute-start.1 = (bf16[12,2,32,256]{3,0,2,1:T(8,128)(2,1)S(1)}, bf16[12,2,32,256]{3,0,2,1:T(8,128)(2,1)}, u32[]{:S(2)}, u32[]{:S(2)}) collective-permute-start(bf16[12,2,32,256]{3,0,2,1:T(8,128)(2,1)S(1)} %copy.171), channel_id=1, source_target_pairs={{2,0},{4,2},{6,4},{8,6},{10,8},{12,10},{14,12},{16,14},{18,16},{20... | collective-permute-start | bytes 1179656 | tf_op jit(solution)/shard_map/ppermute | solution.py:25
  24.0 1.3 copy-start.5
  25.4 5.0 %collective-permute-start.3 = (bf16[12,8,2,256]{3,0,2,1:T(8,128)(2,1)S(1)}, bf16[12,8,2,256]{3,0,2,1:T(8,128)(2,1)S(1)}, u32[]{:S(2)}, u32[]{:S(2)}) collective-permute-start(bf16[12,8,2,256]{3,0,2,1:T(8,128)(2,1)S(1)} %get-tuple-element.49), channel_id=1, source_target_pairs={{1,0},{0,1},{3,2},{2,3},{5,4},{4,5},{7,6},{6,7},{9,8},{8,9},{11,10... | collective-permute-start | bytes 294920 | tf_op jit(solution)/shard_map/ppermute | solution.py:25
  27.4 5.7 %collective-permute-start.2 = (bf16[12,8,2,256]{3,0,2,1:T(8,128)(2,1)S(1)}, bf16[12,8,2,256]{3,0,2,1:T(8,128)(2,1)S(1)}, u32[]{:S(2)}, u32[]{:S(2)}) collective-permute-start(bf16[12,8,2,256]{3,0,2,1:T(8,128)(2,1)S(1)} %get-tuple-element.51), channel_id=1, source_target_pairs={{0,1},{1,0},{2,3},{3,2},{4,5},{5,4},{6,7},{7,6},{8,9},{9,8},{10,11... | collective-permute-start | bytes 294920 | tf_op jit(solution)/shard_map/ppermute | solution.py:22
  33.1 8.4 %collective-permute-start.4 = (bf16[12,8,4,256]{3,0,2,1:T(8,128)(2,1)S(1)}, bf16[12,8,4,256]{3,0,2,1:T(8,128)(2,1)S(1)}, u32[]{:S(2)}, u32[]{:S(2)}) collective-permute-start(bf16[12,8,4,256]{3,0,2,1:T(8,128)(2,1)S(1)} %pad_maximum_fusion.12), channel_id=1, source_target_pairs={{0,2},{1,3},{2,0},{3,1},{4,6},{5,7},{6,4},{7,5},{8,10},{9,11},{10,... | collective-permute-start | bytes 589832 | tf_op jit(solution)/shard_map/ppermute | solution.py:13
  37.0 1.4 copy-start.2
  37.2 2.9 %copy-start.4 = (bf16[12,2,36,256]{3,0,2,1:T(8,128)(2,1)}, bf16[12,2,36,256]{3,0,2,1:T(8,128)(2,1)S(1)}, u32[]{:S(2)}) copy-start(bf16[12,2,36,256]{3,0,2,1:T(8,128)(2,1)S(1)} %get-tuple-element.38) | copy-start | bytes 1327108
  37.2 4.3 %copy-start.9 = (bf16[12,2,36,256]{3,0,2,1:T(8,128)(2,1)}, bf16[12,2,36,256]{3,0,2,1:T(8,128)(2,1)S(1)}, u32[]{:S(2)}) copy-start(bf16[12,2,36,256]{3,0,2,1:T(8,128)(2,1)S(1)} %get-tuple-element.37) | copy-start | bytes 1327108
  40.1 33.3 %collective-permute-start.8 = (bf16[12,4,36,256]{3,1,2,0:T(4,128)(2,1)}, bf16[12,4,36,256]{3,1,2,0:T(4,128)(2,1)}, u32[]{:S(2)}, u32[]{:S(2)}) collective-permute-start(bf16[12,4,36,256]{3,1,2,0:T(4,128)(2,1)} %copy.94), channel_id=1, source_target_pairs={{0,1},{1,0},{2,3},{3,2},{4,5},{5,4},{6,7},{7,6},{8,9},{9,8},{10,11... | collective-permute-start | bytes 2654216 | tf_op jit(solution)/shard_map/ppermute | solution.py:13
  41.5 8.4 %collective-permute-start.5 = (bf16[12,8,4,256]{3,0,2,1:T(8,128)(2,1)S(1)}, bf16[12,8,4,256]{3,0,2,1:T(8,128)(2,1)S(1)}, u32[]{:S(2)}, u32[]{:S(2)}) collective-permute-start(bf16[12,8,4,256]{3,0,2,1:T(8,128)(2,1)S(1)} %collective-permute-done.4), channel_id=1, source_target_pairs={{0,4},{1,5},{2,6},{3,7},{4,0},{5,1},{6,2},{7,3},{8,12},{9,13},{10,... | collective-permute-start | bytes 589832 | tf_op jit(solution)/shard_map/ppermute | solution.py:13
  43.2 39.9 %copy-start.21 = (pred[36]{0:T(512)(128)(4,1)}, pred[36]{0:T(512)(128)(4,1)S(1)}, u32[]{:S(2)}) copy-start(pred[36]{0:T(512)(128)(4,1)S(1)} %or_not_fusion) | copy-start | bytes 112
  49.9 7.9 %collective-permute-start.6 = (bf16[12,8,4,256]{3,0,2,1:T(8,128)(2,1)S(1)}, bf16[12,8,4,256]{3,0,2,1:T(8,128)(2,1)S(1)}, u32[]{:S(2)}, u32[]{:S(2)}) collective-permute-start(bf16[12,8,4,256]{3,0,2,1:T(8,128)(2,1)S(1)} %collective-permute-done.5), channel_id=1, source_target_pairs={{0,8},{1,9},{2,10},{3,11},{4,12},{5,13},{6,14},{7,15},{8,0},{9,1},... | collective-permute-start | bytes 589832 | tf_op jit(solution)/shard_map/ppermute | solution.py:13
  57.7 14.0 %collective-permute-start.7 = (bf16[12,8,4,256]{3,0,2,1:T(8,128)(2,1)S(1)}, bf16[12,8,4,256]{3,0,2,1:T(8,128)(2,1)}, u32[]{:S(2)}, u32[]{:S(2)}) collective-permute-start(bf16[12,8,4,256]{3,0,2,1:T(8,128)(2,1)S(1)} %collective-permute-done.6), channel_id=1, source_target_pairs={{0,16},{1,17},{2,18},{3,19},{4,20},{5,21},{6,22},{7,23},{8,24},{9,... | collective-permute-start | bytes 589832 | tf_op jit(solution)/shard_map/ppermute | solution.py:13
  87.3 0.9 copy-start.15
  87.3 1.0 copy-start.16
  90.7 2.8 copy-start.14
  90.7 2.8 copy-start.18
  96.1 8.7 %copy-start.22 = (pred[36]{0:T(512)(128)(4,1)S(1)}, pred[36]{0:T(512)(128)(4,1)}, u32[]{:S(2)}) copy-start(pred[36]{0:T(512)(128)(4,1)} %copy-done.21) | copy-start | bytes 112
  104.7 5.2 %copy-start.6 = (f32[48,8,2,256]{3,0,2,1:T(8,128)}, f32[48,8,2,256]{3,0,2,1:T(8,128)S(1)}, u32[]{:S(2)}) copy-start(f32[48,8,2,256]{3,0,2,1:T(8,128)S(1)} %fusion.78) | copy-start | bytes 2359300
  110.0 1.4 copy-start.8
  111.5 5.8 %collective-permute-start.9 = (bf16[12,8,4,256]{3,0,2,1:T(8,128)(2,1)S(1)}, bf16[12,8,4,256]{3,0,2,1:T(8,128)(2,1)}, u32[]{:S(2)}, u32[]{:S(2)}) collective-permute-start(bf16[12,8,4,256]{3,0,2,1:T(8,128)(2,1)S(1)} %pad_maximum_fusion.13), channel_id=1, source_target_pairs={{0,2},{1,3},{2,0},{3,1},{4,6},{5,7},{6,4},{7,5},{8,10},{9,11},{10,... | collective-permute-start | bytes 589832 | tf_op jit(solution)/shard_map/ppermute | solution.py:13
  113.6 2.4 copy-start.13
  115.4 34.0 %collective-permute-start.13 = (bf16[12,4,36,256]{3,1,2,0:T(4,128)(2,1)}, bf16[12,4,36,256]{3,1,2,0:T(4,128)(2,1)}, u32[]{:S(2)}, u32[]{:S(2)}) collective-permute-start(bf16[12,4,36,256]{3,1,2,0:T(4,128)(2,1)} %copy.99), channel_id=1, source_target_pairs={{0,1},{1,0},{2,3},{3,2},{4,5},{5,4},{6,7},{7,6},{8,9},{9,8},{10,11... | collective-permute-start | bytes 2654216 | tf_op jit(solution)/shard_map/ppermute | solution.py:13
  116.0 2.4 copy-start.12
  117.3 8.6 %collective-permute-start.10 = (bf16[12,8,4,256]{3,0,2,1:T(8,128)(2,1)}, bf16[12,8,4,256]{3,0,2,1:T(8,128)(2,1)S(1)}, u32[]{:S(2)}, u32[]{:S(2)}) collective-permute-start(bf16[12,8,4,256]{3,0,2,1:T(8,128)(2,1)} %collective-permute-done.9), channel_id=1, source_target_pairs={{0,4},{1,5},{2,6},{3,7},{4,0},{5,1},{6,2},{7,3},{8,12},{9,13},{10,... | collective-permute-start | bytes 589832 | tf_op jit(solution)/shard_map/ppermute | solution.py:13
  118.4 1.2 copy-start.7
  118.4 8.1 %copy-start.10 = (bf16[12,4,32,256]{3,0,2,1:T(8,128)(2,1)S(1)}, bf16[12,4,32,256]{3,0,2,1:T(8,128)(2,1)}, u32[]{:S(2)}) copy-start(bf16[12,4,32,256]{3,0,2,1:T(8,128)(2,1)} %get-tuple-element.54) | copy-start | bytes 2359300
  125.9 7.7 %collective-permute-start.11 = (bf16[12,8,4,256]{3,0,2,1:T(8,128)(2,1)S(1)}, bf16[12,8,4,256]{3,0,2,1:T(8,128)(2,1)S(1)}, u32[]{:S(2)}, u32[]{:S(2)}) collective-permute-start(bf16[12,8,4,256]{3,0,2,1:T(8,128)(2,1)S(1)} %collective-permute-done.10), channel_id=1, source_target_pairs={{0,8},{1,9},{2,10},{3,11},{4,12},{5,13},{6,14},{7,15},{8,0},{9,1},... | collective-permute-start | bytes 589832 | tf_op jit(solution)/shard_map/ppermute | solution.py:13
  126.5 9.4 %copy-start.11 = (bf16[12,4,32,256]{3,0,2,1:T(8,128)(2,1)S(1)}, bf16[12,4,32,256]{3,0,2,1:T(8,128)(2,1)}, u32[]{:S(2)}) copy-start(bf16[12,4,32,256]{3,0,2,1:T(8,128)(2,1)} %get-tuple-element.39) | copy-start | bytes 2359300
  133.6 15.8 %collective-permute-start.12 = (bf16[12,8,4,256]{3,0,2,1:T(8,128)(2,1)S(1)}, bf16[12,8,4,256]{3,0,2,1:T(8,128)(2,1)S(1)}, u32[]{:S(2)}, u32[]{:S(2)}) collective-permute-start(bf16[12,8,4,256]{3,0,2,1:T(8,128)(2,1)S(1)} %collective-permute-done.11), channel_id=1, source_target_pairs={{0,16},{1,17},{2,18},{3,19},{4,20},{5,21},{6,22},{7,23},{8,24},{9,... | collective-permute-start | bytes 589832 | tf_op jit(solution)/shard_map/ppermute | solution.py:13
  151.7 3.9 %slice-start = ((s8[4718592]{0:T(1024)(128)(4,1)}), s8[4194304]{0:T(1024)(128)(4,1)S(1)}, s32[]{:S(2)}) async-start(s8[4718592]{0:T(1024)(128)(4,1)} %bitcast.111), calls=%async_computation.1 | async-start | bytes 8388608
  151.7 4.0 %slice-start.1 = ((s8[4718592]{0:T(1024)(128)(4,1)}), s8[524288]{0:T(1024)(128)(4,1)S(1)}, s32[]{:S(2)}) async-start(s8[4718592]{0:T(1024)(128)(4,1)} %bitcast.111), calls=%async_computation.2 | async-start | bytes 1048576
  158.7 48.6 %collective-permute-start.15 = (bf16[12,2,36,256]{3,1,2,0:T(2,128)(2,1)}, bf16[12,2,36,256]{3,1,2,0:T(2,128)(2,1)S(1)}, u32[]{:S(2)}, u32[]{:S(2)}) collective-permute-start(bf16[12,2,36,256]{3,1,2,0:T(2,128)(2,1)} %copy.103), channel_id=1, source_target_pairs={{2,0},{4,2},{6,4},{8,6},{10,8},{12,10},{14,12},{16,14},{18,16},{20... | collective-permute-start | bytes 1327112 | tf_op jit(solution)/shard_map/ppermute | solution.py:25
  164.1 43.3 %collective-permute-start.14 = (bf16[12,2,36,256]{3,1,2,0:T(2,128)(2,1)}, bf16[12,2,36,256]{3,1,2,0:T(2,128)(2,1)}, u32[]{:S(2)}, u32[]{:S(2)}) collective-permute-start(bf16[12,2,36,256]{3,1,2,0:T(2,128)(2,1)} %copy.102), channel_id=1, source_target_pairs={{0,2},{2,4},{4,6},{6,8},{8,10},{10,12},{12,14},{14,16},{16,18},{18... | collective-permute-start | bytes 1327112 | tf_op jit(solution)/shard_map/ppermute | solution.py:22
  209.4 66.4 %collective-permute-start.16 = (bf16[12,12,2,256]{3,0,2,1:T(8,128)(2,1)}, bf16[12,12,2,256]{3,0,2,1:T(8,128)(2,1)}, u32[]{:S(2)}, u32[]{:S(2)}) collective-permute-start(bf16[12,12,2,256]{3,0,2,1:T(8,128)(2,1)} %get-tuple-element.26), channel_id=1, source_target_pairs={{0,1},{1,0},{2,3},{3,2},{4,5},{5,4},{6,7},{7,6},{8,9},{9,8},{10,11... | collective-permute-start | bytes 442376 | tf_op jit(solution)/shard_map/ppermute | solution.py:22
  211.6 64.1 %collective-permute-start.17 = (bf16[12,12,2,256]{3,0,2,1:T(8,128)(2,1)}, bf16[12,12,2,256]{3,0,2,1:T(8,128)(2,1)}, u32[]{:S(2)}, u32[]{:S(2)}) collective-permute-start(bf16[12,12,2,256]{3,0,2,1:T(8,128)(2,1)} %get-tuple-element.27), channel_id=1, source_target_pairs={{1,0},{0,1},{3,2},{2,3},{5,4},{4,5},{7,6},{6,7},{9,8},{8,9},{11,10... | collective-permute-start | bytes 442376 | tf_op jit(solution)/shard_map/ppermute | solution.py:25
  278.7 0.7 copy-start.20
  279.3 0.9 copy-start.19
  280.2 1.5 copy-start.1
Sparse Core Ops, SparseCore 0:
  137.3 135.0 all-reduce.7
where the time goes:
time: 289 us; the launch traced here: 288 us
  waiting for transfers between devices  118 us (41%)
  blocking collectives  42.6 us (15%)
  local copies, waits for them, and re-layouts  37.7 us (13%)
  starting transfers between devices  28.4 us (10%)
  matrix products  24.5 us (8%)
  other arithmetic  23.1 us (8%)
  between operations  14.6 us (5%)
    psum x1, waiting for transfers between devices, local(): lax.psum((kernel_local, bias_local), ('frow', 'fcol'))  60.8 us
    ppermute x10, waiting for transfers between devices, from_partner(): lax.ppermute(value, axis, [(i, i ^ 1 << distance) for i in range(lax.axis...  44.4 us
    psum x1, blocking collectives, local(): lax.psum((kernel_local, bias_local), ('frow', 'fcol'))  42.6 us
    ppermute x10, starting transfers between devices, from_partner(): lax.ppermute(value, axis, [(i, i ^ 1 << distance) for i in range(lax.axis...  14.2 us
    unnamed x59, local copies, waits for them, and re-layouts  11.3 us
    ppermute x4, starting transfers between devices, with_halo(): lax.ppermute(lax.slice_in_dim(block, 0, width, axis=dim), axis, backward)  11.2 us
    ppermute x4, waiting for transfers between devices, with_halo(): lax.ppermute(lax.slice_in_dim(block, block.shape[dim] - width, None, axis...  9.43 us
    conv_general_dilated x1, matrix products, local(): lax.conv_general_dilated(preactivation_gradient, rotated_strip, (1, 1), (...  8.28 us
  transfers between devices with their start and end apart: 19, of which 10 were waited for; matrix products, arithmetic and copies ran while one was open for 13% of the time, Pallas kernels for 0%

commit v1 on v0

--- a/solution.py
+++ b/solution.py
@@ -7,6 +7,11 @@
 DILATION_STEP = 2
 half_root = 0.7071067811865476
 density_scale = 0.3989422804014327
+
+
+def one_after_other(array, inner_axis, outer_axis):
+    inner = lax.psum(array, inner_axis)
+    return lax.psum(inner, outer_axis)
 
 
 def from_partner(value, axis, distance):
@@ -189,7 +194,7 @@
             )
     kernel_local = jnp.stack(tap_list, 0).reshape(kernel.shape)
     bias_local = jnp.sum(preactivation_gradient.astype(jnp.float32), axis=(0, 1, 2))
-    kernel_total, bias_total = lax.psum((kernel_local, bias_local), ("frow", "fcol"))
+    kernel_total, bias_total = one_after_other((kernel_local, bias_local), "fcol", "frow")
     scale = 1.0 / math.sqrt(
         face_count * tile_rows * lax.axis_size("frow") * tile_cols * lax.axis_size("fcol")
     )

time: 289 us -> 328 us (1.13)
  waiting for transfers between devices: 118 us -> 160 us
  blocking collectives: 42.6 us -> 38.1 us
    psum x1 -> x2, waiting for transfers between devices: 60.8 us -> 99.7 us  [the longest x1 96.6 us: one_after_other(): return lax.psum(inner, outer_axis)]
    psum x1 -> x2, blocking collectives: 42.6 us -> 38.1 us  [the longest x1 33.2 us: one_after_other(): return lax.psum(inner, outer_axis)]
    unnamed x59 -> x63, local copies, waits for them, and re-layouts: 11.3 us -> 11.6 us
  transfers between devices with their start and end apart: 19 -> 20, of which waited for: 10 -> 13; matrix products, arithmetic and copies ran while one was open for 13% -> 12% of each run, Pallas kernels for 0% -> 0%
where the time goes in v1:
time: 328 us; the launch traced here: 327 us
  waiting for transfers between devices  160 us (49%)
  blocking collectives  38.1 us (12%)
  local copies, waits for them, and re-layouts  37.9 us (12%)
  starting transfers between devices  27.3 us (8%)
  other arithmetic  25 us (8%)
  matrix products  24.5 us (7%)
  between operations  14.6 us (4%)
    psum x1, waiting for transfers between devices, one_after_other(): return lax.psum(inner, outer_axis)  96.6 us
    ppermute x10, waiting for transfers between devices, from_partner(): lax.ppermute(value, axis, [(i, i ^ 1 << distance) for i in range(lax.axis...  42.1 us
    psum x1, blocking collectives, one_after_other(): return lax.psum(inner, outer_axis)  33.2 us
    ppermute x10, starting transfers between devices, from_partner(): lax.ppermute(value, axis, [(i, i ^ 1 << distance) for i in range(lax.axis...  14 us
    ppermute x4, waiting for transfers between devices, with_halo(): lax.ppermute(lax.slice_in_dim(block, block.shape[dim] - width, None, axis...  12.6 us
    unnamed x63, local copies, waits for them, and re-layouts  11.6 us
    ppermute x4, starting transfers between devices, with_halo(): lax.ppermute(lax.slice_in_dim(block, 0, width, axis=dim), axis, backward)  11.2 us
    conv_general_dilated x1, matrix products, local(): lax.conv_general_dilated(preactivation_gradient, rotated_strip, (1, 1), (...  8.29 us
  transfers between devices with their start and end apart: 20, of which 13 were waited for; matrix products, arithmetic and copies ran while one was open for 12% of the time, Pallas kernels for 0%

profile of v1, /device:TPU:0, one launch (start us, length us, event | category | flops | bytes accessed | tf_op | source)
XLA Modules:
  0.0 327.4 jit_solution(18216742681642354880)
XLA Ops:
  7.2 1.3 fusion.113
  9.5 5.1 %collective-permute-start.1 = (bf16[12,2,32,256]{3,0,2,1:T(8,128)(2,1)S(1)}, bf16[12,2,32,256]{3,0,2,1:T(8,128)(2,1)S(1)}, u32[]{:S(2)}, u32[]{:S(2)}) collective-permute-start(bf16[12,2,32,256]{3,0,2,1:T(8,128)(2,1)S(1)} %copy.171), channel_id=1, source_target_pairs={{2,0},{4,2},{6,4},{8,6},{10,8},{12,10},{14,12},{16,14},{18,16},{20... | collective-permute-start | bytes 1179656 | tf_op jit(solution)/shard_map/ppermute | solution.py:30
  14.6 6.8 %collective-permute-done = bf16[12,2,32,256]{3,0,2,1:T(8,128)(2,1)} collective-permute-done((bf16[12,2,32,256]{3,0,2,1:T(8,128)(2,1)S(1)}, bf16[12,2,32,256]{3,0,2,1:T(8,128)(2,1)}, u32[]{:S(2)}, u32[]{:S(2)}) %collective-permute-start) | collective-permute-done | bytes 393248 | tf_op jit(solution)/shard_map/ppermute | solution.py:27
  21.4 1.1 constant_dynamic-update-slice_fusion.2
  23.0 1.3 copy-done.5
  24.3 2.0 collective-permute-start.3
  26.5 2.9 collective-permute-done.3
  29.4 2.8 collective-permute-done.2
  32.2 1.8 collective-permute-start.4
  34.0 1.9 pad_maximum_fusion.1
  36.3 1.1 copy-done.2
  37.4 1.6 copy.94
  39.0 1.4 collective-permute-start.8
  40.4 1.7 collective-permute-start.5
  42.2 6.7 %collective-permute-done.5 = bf16[12,8,4,256]{3,0,2,1:T(8,128)(2,1)S(1)} collective-permute-done((bf16[12,8,4,256]{3,0,2,1:T(8,128)(2,1)S(1)}, bf16[12,8,4,256]{3,0,2,1:T(8,128)(2,1)S(1)}, u32[]{:S(2)}, u32[]{:S(2)}) %collective-permute-start.5) | collective-permute-done | bytes 196640 | tf_op jit(solution)/shard_map/ppermute | solution.py:18
  48.9 1.6 collective-permute-start.6
  50.4 6.3 %collective-permute-done.6 = bf16[12,8,4,256]{3,0,2,1:T(8,128)(2,1)S(1)} collective-permute-done((bf16[12,8,4,256]{3,0,2,1:T(8,128)(2,1)S(1)}, bf16[12,8,4,256]{3,0,2,1:T(8,128)(2,1)S(1)}, u32[]{:S(2)}, u32[]{:S(2)}) %collective-permute-start.6) | collective-permute-done | bytes 196640 | tf_op jit(solution)/shard_map/ppermute | solution.py:18
  56.7 2.8 collective-permute-start.7
  60.1 1.3 slice.305
  61.5 1.9 rev.53
  63.4 7.3 %collective-permute-done.7 = bf16[12,8,4,256]{3,0,2,1:T(8,128)(2,1)} collective-permute-done((bf16[12,8,4,256]{3,0,2,1:T(8,128)(2,1)S(1)}, bf16[12,8,4,256]{3,0,2,1:T(8,128)(2,1)}, u32[]{:S(2)}, u32[]{:S(2)}) %collective-permute-start.7) | collective-permute-done | bytes 196640 | tf_op jit(solution)/shard_map/ppermute | solution.py:18
  70.7 1.0 fusion.114
  72.4 3.0 fusion.111
  75.3 0.9 copy.130
  76.3 1.9 rev.54
  78.2 1.9 copy.131
  80.1 1.9 rev.55
  82.0 2.7 broadcast_select_fusion.1
  84.7 1.2 pad_maximum_fusion.6
  87.5 2.1 pad_maximum_fusion.5
  89.6 2.8 fusion.5
  92.4 2.6 convert_reduce_fusion
  95.0 8.3 %fusion.115 = (f32[12,8,36,256]{3,0,2,1:T(8,128)}, bf16[12,8,36,256]{3,0,2,1:T(8,128)(2,1)S(1)}) fusion(bf16[3,3,256,256]{3,2,1,0:T(8,128)(2,1)S(1)} %copy-done, bf16[12,4,32,256]{3,2,1,0:T(8,128)(2,1)S(1)} %get-tuple-element.21), kind=kOutput, calls=%fused_computation.189 | convolution fusion | flops 1813708800 | bytes 7274496 | tf_op jit(solution)/shard_map/conv_general_dilated | solution.py:205
  103.7 2.6 fusion.60
  108.9 1.4 copy-done.6
  111.1 2.0 fusion.108
  113.2 0.9 rev.76
  114.1 1.3 pad_maximum_fusion.4
  115.4 1.6 copy.99
  117.6 1.2 fusion.37
  118.8 1.1 collective-permute-start.10
  119.9 1.2 fusion.36
  121.2 6.3 %collective-permute-done.10 = bf16[12,8,4,256]{3,0,2,1:T(8,128)(2,1)S(1)} collective-permute-done((bf16[12,8,4,256]{3,0,2,1:T(8,128)(2,1)}, bf16[12,8,4,256]{3,0,2,1:T(8,128)(2,1)S(1)}, u32[]{:S(2)}, u32[]{:S(2)}) %collective-permute-start.10) | collective-permute-done | bytes 196640 | tf_op jit(solution)/shard_map/ppermute | solution.py:18
  128.1 1.2 fusion.35
  129.3 5.9 %collective-permute-done.11 = bf16[12,8,4,256]{3,0,2,1:T(8,128)(2,1)S(1)} collective-permute-done((bf16[12,8,4,256]{3,0,2,1:T(8,128)(2,1)S(1)}, bf16[12,8,4,256]{3,0,2,1:T(8,128)(2,1)S(1)}, u32[]{:S(2)}, u32[]{:S(2)}) %collective-permute-start.11) | collective-permute-done | bytes 196640 | tf_op jit(solution)/shard_map/ppermute | solution.py:18
  135.2 2.4 collective-permute-start.12
  137.6 1.2 fusion.34
  138.9 9.8 %collective-permute-done.12 = bf16[12,8,4,256]{3,0,2,1:T(8,128)(2,1)S(1)} collective-permute-done((bf16[12,8,4,256]{3,0,2,1:T(8,128)(2,1)S(1)}, bf16[12,8,4,256]{3,0,2,1:T(8,128)(2,1)S(1)}, u32[]{:S(2)}, u32[]{:S(2)}) %collective-permute-start.12) | collective-permute-done | bytes 196640 | tf_op jit(solution)/shard_map/ppermute | solution.py:18
  148.7 2.2 fusion.110
  151.0 3.5 %slice_select_fusion.3 = (f32[12,2,36,256]{3,0,2,1:T(8,128)S(1)}, f32[12,2,36,256]{3,0,2,1:T(8,128)S(1)}, f32[12,2,36,256]{3,0,2,1:T(8,128)S(1)}) fusion(f32[12,8,36,256]{3,0,2,1:T(8,128)} %get-tuple-element.70, f32[48,2,36,256]{3,0,2,1:T(8,128)} %fusion.60, bf16[12,2,36,256]{3,1,2,0:T(2,128)(2,1)S(1)} %get-tuple-element.57, pred[]{:T(512)S(6)} %eq.57, ...), kind=kLoop, calls=%fused_computation.53 | loop fusion | flops 884736 | bytes 6635522 | tf_op jit(solution)/shard_map/jit(_where)/select_n | solution.py:248
  157.2 1.2 copy.103
  158.4 3.6 %collective-permute-start.15 = (bf16[12,2,36,256]{3,1,2,0:T(2,128)(2,1)}, bf16[12,2,36,256]{3,1,2,0:T(2,128)(2,1)S(1)}, u32[]{:S(2)}, u32[]{:S(2)}) collective-permute-start(bf16[12,2,36,256]{3,1,2,0:T(2,128)(2,1)} %copy.103), channel_id=1, source_target_pairs={{2,0},{4,2},{6,4},{8,6},{10,8},{12,10},{14,12},{16,14},{18,16},{20... | collective-permute-start | bytes 1327112 | tf_op jit(solution)/shard_map/ppermute | solution.py:30
  161.9 1.2 copy.102
  163.2 5.0 %psum.30 = f32[256]{0:T(256)S(1)} all-reduce(f32[256]{0:T(256)S(1)} %get-tuple-element.20), channel_id=1, replica_groups=mesh['frow'=16,'fcol'=2] {'fcol'}, use_global_device_ids=true, to_apply=%region_3.4 | all-reduce | flops 256 | bytes 2048 | tf_op jit(solution)/shard_map/psum | solution.py:13
  168.2 33.2 %psum.31 = f32[256]{0:T(256)S(1)} all-reduce(f32[256]{0:T(256)S(1)} %psum.30), channel_id=1, replica_groups=mesh['frow'=16,'fcol'=2] {'frow'}, use_global_device_ids=true, to_apply=%region_4.5 | all-reduce | flops 256 | bytes 2048 | tf_op jit(solution)/shard_map/psum | solution.py:14
  201.4 1.1 copy.104
  203.4 1.4 collective-permute-start.16
  206.0 3.1 all-reduce.9.cloned.1.call-done
  209.1 3.1 collective-permute-done.16
  212.2 2.6 collective-permute-done.17
  214.8 2.9 maximum_convert_fusion
  219.6 1.1 copy.115
  220.7 96.6 %all-reduce.11.cloned.1.call-done = f32[3,3,256,256]{3,2,1,0:T(8,128)} async-done(((f32[3,3,256,256]{3,2,1,0:T(8,128)}), f32[3,3,256,256]{3,2,1,0:T(8,128)}) %all-reduce.11.cloned.1.call-update) | async-done | bytes 2359312 | tf_op jit(solution)/shard_map/psum | solution.py:14
  317.3 3.3 broadcast_multiply_fusion
  (118 shorter events, 16.7 us)
Async XLA Ops:
  7.2 82.4 %copy-start = (bf16[3,3,256,256]{3,2,1,0:T(8,128)(2,1)S(1)}, bf16[3,3,256,256]{3,2,1,0:T(8,128)(2,1)}, u32[]{:S(2)}) copy-start(bf16[3,3,256,256]{3,2,1,0:T(8,128)(2,1)} %param.6) | copy-start | bytes 3538948
  7.2 15.3 %copy-start.3 = (bf16[12,4,32,256]{3,2,1,0:T(8,128)(2,1)S(1)}, bf16[12,4,32,256]{3,2,1,0:T(8,128)(2,1)}, u32[]{:S(2)}) copy-start(bf16[12,4,32,256]{3,2,1,0:T(8,128)(2,1)} %param.5) | copy-start | bytes 2359300
  7.2 201.9 %all-reduce.9.cloned.1.call-start = ((), (), s32[]{:S(2)}) async-start(), calls=%async_computation | async-start | bytes 4718592 | tf_op jit(solution)/shard_map/psum | solution.py:13
  8.8 12.6 %collective-permute-start = (bf16[12,2,32,256]{3,0,2,1:T(8,128)(2,1)S(1)}, bf16[12,2,32,256]{3,0,2,1:T(8,128)(2,1)}, u32[]{:S(2)}, u32[]{:S(2)}) collective-permute-start(bf16[12,2,32,256]{3,0,2,1:T(8,128)(2,1)S(1)} %copy.170), channel_id=1, source_target_pairs={{0,2},{2,4},{4,6},{6,8},{8,10},{10,12},{12,14},{14,16},{16,18},{18... | collective-permute-start | bytes 1179656 | tf_op jit(solution)/shard_map/ppermute | solution.py:27
  9.5 16.9 %copy-start.19 = (s32[12,4,3]{0,1,2:T(4,128)S(1)}, s32[12,4,3]{0,1,2:T(4,128)}, u32[]{:S(2)}) copy-start(s32[12,4,3]{0,1,2:T(4,128)} %param.9) | copy-start | bytes 1732
  9.5 13.4 %collective-permute-start.1 = (bf16[12,2,32,256]{3,0,2,1:T(8,128)(2,1)S(1)}, bf16[12,2,32,256]{3,0,2,1:T(8,128)(2,1)S(1)}, u32[]{:S(2)}, u32[]{:S(2)}) collective-permute-start(bf16[12,2,32,256]{3,0,2,1:T(8,128)(2,1)S(1)} %copy.171), channel_id=1, source_target_pairs={{2,0},{4,2},{6,4},{8,6},{10,8},{12,10},{14,12},{16,14},{18,16},{20... | collective-permute-start | bytes 1179656 | tf_op jit(solution)/shard_map/ppermute | solution.py:30
  23.0 1.3 copy-start.5
  24.3 5.0 %collective-permute-start.3 = (bf16[12,8,2,256]{3,0,2,1:T(8,128)(2,1)S(1)}, bf16[12,8,2,256]{3,0,2,1:T(8,128)(2,1)S(1)}, u32[]{:S(2)}, u32[]{:S(2)}) collective-permute-start(bf16[12,8,2,256]{3,0,2,1:T(8,128)(2,1)S(1)} %get-tuple-element.49), channel_id=1, source_target_pairs={{1,0},{0,1},{3,2},{2,3},{5,4},{4,5},{7,6},{6,7},{9,8},{8,9},{11,10... | collective-permute-start | bytes 294920 | tf_op jit(solution)/shard_map/ppermute | solution.py:30
  26.3 5.8 %collective-permute-start.2 = (bf16[12,8,2,256]{3,0,2,1:T(8,128)(2,1)S(1)}, bf16[12,8,2,256]{3,0,2,1:T(8,128)(2,1)S(1)}, u32[]{:S(2)}, u32[]{:S(2)}) collective-permute-start(bf16[12,8,2,256]{3,0,2,1:T(8,128)(2,1)S(1)} %get-tuple-element.51), channel_id=1, source_target_pairs={{0,1},{1,0},{2,3},{3,2},{4,5},{5,4},{6,7},{7,6},{8,9},{9,8},{10,11... | collective-permute-start | bytes 294920 | tf_op jit(solution)/shard_map/ppermute | solution.py:27
  32.2 8.2 %collective-permute-start.4 = (bf16[12,8,4,256]{3,0,2,1:T(8,128)(2,1)S(1)}, bf16[12,8,4,256]{3,0,2,1:T(8,128)(2,1)S(1)}, u32[]{:S(2)}, u32[]{:S(2)}) collective-permute-start(bf16[12,8,4,256]{3,0,2,1:T(8,128)(2,1)S(1)} %pad_maximum_fusion.12), channel_id=1, source_target_pairs={{0,2},{1,3},{2,0},{3,1},{4,6},{5,7},{6,4},{7,5},{8,10},{9,11},{10,... | collective-permute-start | bytes 589832 | tf_op jit(solution)/shard_map/ppermute | solution.py:18
  36.0 1.4 copy-start.2
  36.1 2.9 copy-start.4
  36.1 4.3 %copy-start.7 = (bf16[12,2,36,256]{3,0,2,1:T(8,128)(2,1)}, bf16[12,2,36,256]{3,0,2,1:T(8,128)(2,1)S(1)}, u32[]{:S(2)}) copy-start(bf16[12,2,36,256]{3,0,2,1:T(8,128)(2,1)S(1)} %get-tuple-element.37) | copy-start | bytes 1327108
  39.0 33.3 %collective-permute-start.8 = (bf16[12,4,36,256]{3,1,2,0:T(4,128)(2,1)}, bf16[12,4,36,256]{3,1,2,0:T(4,128)(2,1)}, u32[]{:S(2)}, u32[]{:S(2)}) collective-permute-start(bf16[12,4,36,256]{3,1,2,0:T(4,128)(2,1)} %copy.94), channel_id=1, source_target_pairs={{0,1},{1,0},{2,3},{3,2},{4,5},{5,4},{6,7},{7,6},{8,9},{9,8},{10,11... | collective-permute-start | bytes 2654216 | tf_op jit(solution)/shard_map/ppermute | solution.py:18
  40.4 8.4 %collective-permute-start.5 = (bf16[12,8,4,256]{3,0,2,1:T(8,128)(2,1)S(1)}, bf16[12,8,4,256]{3,0,2,1:T(8,128)(2,1)S(1)}, u32[]{:S(2)}, u32[]{:S(2)}) collective-permute-start(bf16[12,8,4,256]{3,0,2,1:T(8,128)(2,1)S(1)} %collective-permute-done.4), channel_id=1, source_target_pairs={{0,4},{1,5},{2,6},{3,7},{4,0},{5,1},{6,2},{7,3},{8,12},{9,13},{10,... | collective-permute-start | bytes 589832 | tf_op jit(solution)/shard_map/ppermute | solution.py:18
  42.2 39.9 %copy-start.23 = (pred[36]{0:T(512)(128)(4,1)}, pred[36]{0:T(512)(128)(4,1)S(1)}, u32[]{:S(2)}) copy-start(pred[36]{0:T(512)(128)(4,1)S(1)} %or_not_fusion) | copy-start | bytes 112
  48.9 7.9 %collective-permute-start.6 = (bf16[12,8,4,256]{3,0,2,1:T(8,128)(2,1)S(1)}, bf16[12,8,4,256]{3,0,2,1:T(8,128)(2,1)S(1)}, u32[]{:S(2)}, u32[]{:S(2)}) collective-permute-start(bf16[12,8,4,256]{3,0,2,1:T(8,128)(2,1)S(1)} %collective-permute-done.5), channel_id=1, source_target_pairs={{0,8},{1,9},{2,10},{3,11},{4,12},{5,13},{6,14},{7,15},{8,0},{9,1},... | collective-permute-start | bytes 589832 | tf_op jit(solution)/shard_map/ppermute | solution.py:18
  56.7 14.0 %collective-permute-start.7 = (bf16[12,8,4,256]{3,0,2,1:T(8,128)(2,1)S(1)}, bf16[12,8,4,256]{3,0,2,1:T(8,128)(2,1)}, u32[]{:S(2)}, u32[]{:S(2)}) collective-permute-start(bf16[12,8,4,256]{3,0,2,1:T(8,128)(2,1)S(1)} %collective-permute-done.6), channel_id=1, source_target_pairs={{0,16},{1,17},{2,18},{3,19},{4,20},{5,21},{6,22},{7,23},{8,24},{9,... | collective-permute-start | bytes 589832 | tf_op jit(solution)/shard_map/ppermute | solution.py:18
  86.3 0.9 copy-start.17
  86.3 1.0 copy-start.18
  89.6 2.8 copy-start.16
  89.6 2.8 copy-start.20
  95.0 8.7 %copy-start.24 = (pred[36]{0:T(512)(128)(4,1)S(1)}, pred[36]{0:T(512)(128)(4,1)}, u32[]{:S(2)}) copy-start(pred[36]{0:T(512)(128)(4,1)} %copy-done.23) | copy-start | bytes 112
  108.9 1.4 copy-start.6
  111.1 7.7 %collective-permute-start.9 = (bf16[12,8,4,256]{3,0,2,1:T(8,128)(2,1)}, bf16[12,8,4,256]{3,0,2,1:T(8,128)(2,1)}, u32[]{:S(2)}, u32[]{:S(2)}) collective-permute-start(bf16[12,8,4,256]{3,0,2,1:T(8,128)(2,1)} %pad_maximum_fusion.13), channel_id=1, source_target_pairs={{0,2},{1,3},{2,0},{3,1},{4,6},{5,7},{6,4},{7,5},{8,10},{9,11},{10,... | collective-permute-start | bytes 589832 | tf_op jit(solution)/shard_map/ppermute | solution.py:18
  114.1 3.5 %copy-start.15 = (bf16[12,4,32,256]{3,0,2,1:T(8,128)(2,1)S(1)}, bf16[12,4,32,256]{3,0,2,1:T(8,128)(2,1)}, u32[]{:S(2)}) copy-start(bf16[12,4,32,256]{3,0,2,1:T(8,128)(2,1)} %get-tuple-element.41) | copy-start | bytes 2359300
  117.0 31.8 %collective-permute-start.13 = (bf16[12,4,36,256]{3,1,2,0:T(4,128)(2,1)}, bf16[12,4,36,256]{3,1,2,0:T(4,128)(2,1)}, u32[]{:S(2)}, u32[]{:S(2)}) collective-permute-start(bf16[12,4,36,256]{3,1,2,0:T(4,128)(2,1)} %copy.99), channel_id=1, source_target_pairs={{0,1},{1,0},{2,3},{3,2},{4,5},{5,4},{6,7},{7,6},{8,9},{9,8},{10,11... | collective-permute-start | bytes 2654216 | tf_op jit(solution)/shard_map/ppermute | solution.py:18
  117.6 2.4 copy-start.14
  118.8 8.6 %collective-permute-start.10 = (bf16[12,8,4,256]{3,0,2,1:T(8,128)(2,1)}, bf16[12,8,4,256]{3,0,2,1:T(8,128)(2,1)S(1)}, u32[]{:S(2)}, u32[]{:S(2)}) collective-permute-start(bf16[12,8,4,256]{3,0,2,1:T(8,128)(2,1)} %collective-permute-done.9), channel_id=1, source_target_pairs={{0,4},{1,5},{2,6},{3,7},{4,0},{5,1},{6,2},{7,3},{8,12},{9,13},{10,... | collective-permute-start | bytes 589832 | tf_op jit(solution)/shard_map/ppermute | solution.py:18
  119.9 8.2 %copy-start.12 = (bf16[12,4,32,256]{3,0,2,1:T(8,128)(2,1)S(1)}, bf16[12,4,32,256]{3,0,2,1:T(8,128)(2,1)}, u32[]{:S(2)}) copy-start(bf16[12,4,32,256]{3,0,2,1:T(8,128)(2,1)} %get-tuple-element.54) | copy-start | bytes 2359300
  127.5 7.7 %collective-permute-start.11 = (bf16[12,8,4,256]{3,0,2,1:T(8,128)(2,1)S(1)}, bf16[12,8,4,256]{3,0,2,1:T(8,128)(2,1)S(1)}, u32[]{:S(2)}, u32[]{:S(2)}) collective-permute-start(bf16[12,8,4,256]{3,0,2,1:T(8,128)(2,1)S(1)} %collective-permute-done.10), channel_id=1, source_target_pairs={{0,8},{1,9},{2,10},{3,11},{4,12},{5,13},{6,14},{7,15},{8,0},{9,1},... | collective-permute-start | bytes 589832 | tf_op jit(solution)/shard_map/ppermute | solution.py:18
  128.1 9.5 %copy-start.13 = (bf16[12,4,32,256]{3,0,2,1:T(8,128)(2,1)S(1)}, bf16[12,4,32,256]{3,0,2,1:T(8,128)(2,1)}, u32[]{:S(2)}) copy-start(bf16[12,4,32,256]{3,0,2,1:T(8,128)(2,1)} %get-tuple-element.39) | copy-start | bytes 2359300
  135.2 13.5 %collective-permute-start.12 = (bf16[12,8,4,256]{3,0,2,1:T(8,128)(2,1)S(1)}, bf16[12,8,4,256]{3,0,2,1:T(8,128)(2,1)S(1)}, u32[]{:S(2)}, u32[]{:S(2)}) collective-permute-start(bf16[12,8,4,256]{3,0,2,1:T(8,128)(2,1)S(1)} %collective-permute-done.11), channel_id=1, source_target_pairs={{0,16},{1,17},{2,18},{3,19},{4,20},{5,21},{6,22},{7,23},{8,24},{9,... | collective-permute-start | bytes 589832 | tf_op jit(solution)/shard_map/ppermute | solution.py:18
  138.8 178.5 %all-reduce.11.cloned.1.call-start = ((), (), s32[]{:S(2)}) async-start(), calls=%async_computation.1 | async-start | bytes 4718592 | tf_op jit(solution)/shard_map/psum | solution.py:14
  150.9 3.9 %slice-start = ((s8[4718592]{0:T(1024)(128)(4,1)}), s8[4194304]{0:T(1024)(128)(4,1)S(1)}, s32[]{:S(2)}) async-start(s8[4718592]{0:T(1024)(128)(4,1)} %bitcast.111), calls=%async_computation.2 | async-start | bytes 8388608
  151.0 4.0 %slice-start.1 = ((s8[4718592]{0:T(1024)(128)(4,1)}), s8[524288]{0:T(1024)(128)(4,1)S(1)}, s32[]{:S(2)}) async-start(s8[4718592]{0:T(1024)(128)(4,1)} %bitcast.111), calls=%async_computation.3 | async-start | bytes 1048576
  156.2 0.6 copy-start.8
  156.2 0.7 copy-start.10
  157.2 45.4 %copy-start.9 = (bf16[12,8,2,256]{3,0,2,1:T(8,128)(2,1)S(1)}, bf16[12,8,2,256]{3,0,2,1:T(8,128)(2,1)}, u32[]{:S(2)}) copy-start(bf16[12,8,2,256]{3,0,2,1:T(8,128)(2,1)} %copy-done.8) | copy-start | bytes 294916
  157.2 45.4 %copy-start.11 = (bf16[12,8,2,256]{3,0,2,1:T(8,128)(2,1)S(1)}, bf16[12,8,2,256]{3,0,2,1:T(8,128)(2,1)}, u32[]{:S(2)}) copy-start(bf16[12,8,2,256]{3,0,2,1:T(8,128)(2,1)} %copy-done.10) | copy-start | bytes 294916
  158.4 42.9 %collective-permute-start.15 = (bf16[12,2,36,256]{3,1,2,0:T(2,128)(2,1)}, bf16[12,2,36,256]{3,1,2,0:T(2,128)(2,1)S(1)}, u32[]{:S(2)}, u32[]{:S(2)}) collective-permute-start(bf16[12,2,36,256]{3,1,2,0:T(2,128)(2,1)} %copy.103), channel_id=1, source_target_pairs={{2,0},{4,2},{6,4},{8,6},{10,8},{12,10},{14,12},{16,14},{18,16},{20... | collective-permute-start | bytes 1327112 | tf_op jit(solution)/shard_map/ppermute | solution.py:30
  163.2 38.2 %collective-permute-start.14 = (bf16[12,2,36,256]{3,1,2,0:T(2,128)(2,1)}, bf16[12,2,36,256]{3,1,2,0:T(2,128)(2,1)}, u32[]{:S(2)}, u32[]{:S(2)}) collective-permute-start(bf16[12,2,36,256]{3,1,2,0:T(2,128)(2,1)} %copy.102), channel_id=1, source_target_pairs={{0,2},{2,4},{4,6},{6,8},{8,10},{10,12},{12,14},{14,16},{16,18},{18... | collective-permute-start | bytes 1327112 | tf_op jit(solution)/shard_map/ppermute | solution.py:27
  203.4 8.8 %collective-permute-start.16 = (bf16[12,12,2,256]{3,0,2,1:T(8,128)(2,1)}, bf16[12,12,2,256]{3,0,2,1:T(8,128)(2,1)}, u32[]{:S(2)}, u32[]{:S(2)}) collective-permute-start(bf16[12,12,2,256]{3,0,2,1:T(8,128)(2,1)} %get-tuple-element.26), channel_id=1, source_target_pairs={{0,1},{1,0},{2,3},{3,2},{4,5},{5,4},{6,7},{7,6},{8,9},{9,8},{10,11... | collective-permute-start | bytes 442376 | tf_op jit(solution)/shard_map/ppermute | solution.py:27
  204.8 10.0 %collective-permute-start.17 = (bf16[12,12,2,256]{3,0,2,1:T(8,128)(2,1)}, bf16[12,12,2,256]{3,0,2,1:T(8,128)(2,1)}, u32[]{:S(2)}, u32[]{:S(2)}) collective-permute-start(bf16[12,12,2,256]{3,0,2,1:T(8,128)(2,1)} %get-tuple-element.27), channel_id=1, source_target_pairs={{1,0},{0,1},{3,2},{2,3},{5,4},{4,5},{7,6},{6,7},{9,8},{8,9},{11,10... | collective-permute-start | bytes 442376 | tf_op jit(solution)/shard_map/ppermute | solution.py:30
  217.7 0.7 copy-start.22
  218.4 0.9 copy-start.21
  219.6 101.0 %copy-start.1 = (bf16[3,3,256,256]{3,2,1,0:T(8,128)(2,1)S(1)}, bf16[3,3,256,256]{3,2,1,0:T(8,128)(2,1)}, u32[]{:S(2)}) copy-start(bf16[3,3,256,256]{3,2,1,0:T(8,128)(2,1)} %param.6) | copy-start | bytes 3538948
Sparse Core Ops, SparseCore 0:
  138.9 70.1 all-reduce.8
  213.1 104.1 all-reduce.10
